TPU v7x, 256 devices: a whole 4x4x8 slice. The times are simulated.
256 devices in a mesh: row: 8 (over x, core), col: 32 (over y, z).
Axes of the slice: x: 4, y: 4, z: 8, core: 2. Of those that a mesh axis runs over, the one named last changes fastest.
Arguments:
- upper_panel: float32 [2048, 8192], P('row', 'col')
- lower_panel: float32 [2048, 8192], P('row', 'col')
- pole_values: float32 [2, 8192], P(None, 'col'), may hold values from 0 to 4, as said below
- coupling: float32 [2, 8192], P(None, 'col'), may hold values from -6 to 6
- kept_mask: int32 [2, 8192], P(None, 'col'), may hold values from 0 to 1, as said below
- shifts: float32 [16384], P('col'), may hold values from 0 to 4
- source: int32 [16384], P('col'), may hold values from 0 to 16384, as said below
Outputs:
- vectors: float32 [2, 2048, 16384], P(None, 'row', 'col')
- slab_weight: float32 [16384], P('col')
Inputs may be any that keep to these rules, and one draw needn't show every extreme that they name: source[j] = 16384 marks an undeflated merged column; any other value is the pole whose child column the merged column copies, and no pole is named twice. Each device's 512 merged columns hold from 64 to 384 undeflated columns, and some device holds exactly 384. kept_mask is 0 exactly at the poles named in source. Some device of col holds no deflated pole: every pole of both children that it holds is kept. `pole_values`: every pole lies at least 0.4 / 16384 away from every entry of shifts.
All inputs are finite; a program needn't handle non-finite values.
Results may differ from a plain program's by a relative error of at most 0.0003.
Values sent between devices are 32-bit elements; how exact they have to be, the bound alone decides.
A program may use at most 64 MiB of HBM per device.

v0:
```python
import math
import jax
import jax.numpy as jnp
from jax import lax
from jax.sharding import PartitionSpec as P

N1 = 8192
exact_mode = lax.Precision.HIGHEST


def cauchy_block(pole_vals, weights, shift_vals):
    return weights[:, :, None] / (pole_vals[:, :, None] - shift_vals[None, None, :])


def local(upper_panel, lower_panel, pole_values, coupling, kept_mask, shifts, source):
    rows_here = upper_panel.shape[0]
    own_cols = shifts.shape[0]
    weighted = coupling * kept_mask.astype(jnp.float32)
    undeflated = source == 2 * N1
    child_base = jnp.array([0, N1], jnp.int32)
    zeros_acc = jnp.zeros((rows_here, own_cols), jnp.float32)
    pieces = (
        lax.all_gather(upper_panel, "col", axis=1, tiled=True),
        lax.all_gather(lower_panel, "col", axis=1, tiled=True),
        lax.all_gather(pole_values, "col", axis=1, tiled=True),
        lax.all_gather(weighted, "col", axis=1, tiled=True),
    )
    span_cols = math.gcd(pieces[0].shape[1], 1024)

    def advance(number, running):
        window = [
            lax.dynamic_slice_in_dim(member, number * span_cols, span_cols, 1) for member in pieces
        ]
        first_pole = number * span_cols
        cauchy = cauchy_block(window[2], window[3], shifts)
        indices = first_pole + lax.iota(jnp.int32, span_cols)
        one_hot = indices[None, :, None] + child_base[:, None, None] == source[None, None, :]
        basis_tile = jnp.where(undeflated[None, None, :], cauchy, one_hot.astype(jnp.float32))
        upper_acc = running[0] + jnp.dot(
            window[0], basis_tile[0], precision=exact_mode, preferred_element_type=jnp.float32
        )
        lower_acc = running[1] + jnp.dot(
            window[1], basis_tile[1], precision=exact_mode, preferred_element_type=jnp.float32
        )
        return (upper_acc, lower_acc, running[2] + jnp.sum(cauchy * cauchy, axis=(0, 1)))

    upper_acc, lower_acc, norm_sums = lax.fori_loop(
        0,
        pieces[0].shape[1] // span_cols,
        advance,
        (zeros_acc, zeros_acc, jnp.zeros((own_cols,), jnp.float32)),
    )
    scaling = jnp.where(undeflated, lax.rsqrt(norm_sums), 1.0)
    vectors = jnp.stack([upper_acc * scaling[None, :], lower_acc * scaling[None, :]])
    partial_weight = jnp.sum(vectors * vectors, axis=(0, 1))
    slab_weight = lax.psum(partial_weight, "row") / (2 * rows_here * lax.axis_size("row"))
    return (vectors, slab_weight)


def solution(mesh):
    in_specs = (
        P("row", "col"),
        P("row", "col"),
        P(None, "col"),
        P(None, "col"),
        P(None, "col"),
        P("col"),
        P("col"),
    )
    out_specs = (P(None, "row", "col"), P("col"))
    return jax.shard_map(local, mesh=mesh, in_specs=in_specs, out_specs=out_specs, check_vma=False)
```

profile of v0, /device:TPU:1, one launch (start us, length us, event | category | flops | bytes accessed | tf_op | source)
XLA Modules:
  0.0 310.2 jit_solution(16482954497444541827)
XLA Ops:
  7.2 0.0 all-gather.3.cloned.1.call-start
  7.2 0.7 all-gather.3.cloned.1.call-update
  7.9 0.0 all-gather.5.cloned.1.call-start
  7.9 0.7 all-gather.5.cloned.1.call-update
  8.7 0.7 convert_multiply_fusion
  9.4 41.5 %all_gather.13 = f32[2,8192]{1,0:T(2,128)S(1)} all-gather(f32[2,256]{1,0:T(2,128)S(1)} %convert_multiply_fusion), channel_id=1, replica_groups=mesh['row'=8,'col'=32] {'col'}, dimensions={1}, use_global_device_ids=true | all-gather | bytes 67584 | tf_op jit(solution)/shard_map/all_gather | solution.py:26
  50.9 39.2 %all_gather.14 = f32[2,8192]{1,0:T(2,128)S(1)} all-gather(f32[2,256]{1,0:T(2,128)} %param.12), channel_id=1, replica_groups=mesh['row'=8,'col'=32] {'col'}, dimensions={1}, use_global_device_ids=true | all-gather | bytes 67584 | tf_op jit(solution)/shard_map/all_gather | solution.py:25
  90.1 0.7 broadcast_compare_fusion
  90.8 23.1 %all-gather.3.cloned.1.call-done = f32[256,8192]{1,0:T(8,128)} async-done(((f32[256,256]{1,0:T(8,128)}), f32[256,8192]{1,0:T(8,128)}) %all-gather.3.cloned.1.call-update) | async-done | bytes 8388624 | tf_op jit(solution)/shard_map/all_gather | solution.py:23
  113.9 102.9 %all-gather.5.cloned.1.call-done = f32[256,8192]{1,0:T(8,128)} async-done(((f32[256,256]{1,0:T(8,128)}), f32[256,8192]{1,0:T(8,128)}) %all-gather.5.cloned.1.call-update) | async-done | bytes 8388624 | tf_op jit(solution)/shard_map/all_gather | solution.py:24
  216.8 68.3 %while.18 = (s32[]{:T(128)}, f32[256,512]{1,0:T(8,128)S(1)}, f32[256,512]{1,0:T(8,128)S(1)}, f32[512]{0:T(512)S(1)}, f32[256,8192]{1,0:T(8,128)}, /*index=5*/pre...) while((s32[]{:T(128)}, f32[256,512]{1,0:T(8,128)S(1)}, ...), condition=%wide.region_2.3_spmd.clone, body=%wide.region_0.2_spmd.clone.sunk | while | flops 3229093376 | bytes 12669679 | solution.py:47
  216.9 0.1 broadcast_add_fusion.2
  216.9 1.9 multiply_reduce_fusion.3
  218.8 3.3 %fusion.17 = f32[256,512]{1,0:T(8,128)S(1)} fusion(f32[2,1024,512]{2,1,0:T(8,128)S(1)} %get-tuple-element.347, f32[256,8192]{1,0:T(8,128)} %get-tuple-element.389, s32[]{:T(128)S(6)} %select_n.28, f32[256,512]{1,0:T(8,128)S(1)} %get-tuple-element.366, pred[]{:T(512)S(6)} %compare.3), kind=kOutput, calls=%fused_computation.9.clone.1 | convolution fusion | flops 1610874880 | bytes 4194309 | tf_op jit(solution)/shard_map/while/body/eval_jaxpr/dot_general | solution.py:42
  222.1 3.3 %fusion.16 = f32[256,512]{1,0:T(8,128)S(1)} fusion(f32[2,1024,512]{2,1,0:T(8,128)S(1)} %get-tuple-element.347, f32[256,8192]{1,0:T(8,128)} %get-tuple-element.383, s32[]{:T(128)S(6)} %select_n.28, f32[256,512]{1,0:T(8,128)S(1)} %get-tuple-element.365, pred[]{:T(512)S(6)} %compare.3), kind=kOutput, calls=%fused_computation.8.clone.1 | convolution fusion | flops 1610874880 | bytes 4194309 | tf_op jit(solution)/shard_map/while/body/eval_jaxpr/dot_general | solution.py:39
  225.4 0.1 broadcast_add_fusion.2
  225.5 1.9 multiply_reduce_fusion.3
  227.4 3.3 %fusion.17 = f32[256,512]{1,0:T(8,128)S(1)} fusion(f32[2,1024,512]{2,1,0:T(8,128)S(1)} %get-tuple-element.347, f32[256,8192]{1,0:T(8,128)} %get-tuple-element.389, s32[]{:T(128)S(6)} %select_n.28, f32[256,512]{1,0:T(8,128)S(1)} %get-tuple-element.366, pred[]{:T(512)S(6)} %compare.3), kind=kOutput, calls=%fused_computation.9.clone.1 | convolution fusion | flops 1610874880 | bytes 4194309 | tf_op jit(solution)/shard_map/while/body/eval_jaxpr/dot_general | solution.py:42
  230.6 3.3 %fusion.16 = f32[256,512]{1,0:T(8,128)S(1)} fusion(f32[2,1024,512]{2,1,0:T(8,128)S(1)} %get-tuple-element.347, f32[256,8192]{1,0:T(8,128)} %get-tuple-element.383, s32[]{:T(128)S(6)} %select_n.28, f32[256,512]{1,0:T(8,128)S(1)} %get-tuple-element.365, pred[]{:T(512)S(6)} %compare.3), kind=kOutput, calls=%fused_computation.8.clone.1 | convolution fusion | flops 1610874880 | bytes 4194309 | tf_op jit(solution)/shard_map/while/body/eval_jaxpr/dot_general | solution.py:39
  233.9 0.1 broadcast_add_fusion.2
  234.0 1.9 multiply_reduce_fusion.3
  235.9 3.3 %fusion.17 = f32[256,512]{1,0:T(8,128)S(1)} fusion(f32[2,1024,512]{2,1,0:T(8,128)S(1)} %get-tuple-element.347, f32[256,8192]{1,0:T(8,128)} %get-tuple-element.389, s32[]{:T(128)S(6)} %select_n.28, f32[256,512]{1,0:T(8,128)S(1)} %get-tuple-element.366, pred[]{:T(512)S(6)} %compare.3), kind=kOutput, calls=%fused_computation.9.clone.1 | convolution fusion | flops 1610874880 | bytes 4194309 | tf_op jit(solution)/shard_map/while/body/eval_jaxpr/dot_general | solution.py:42
  239.2 3.3 %fusion.16 = f32[256,512]{1,0:T(8,128)S(1)} fusion(f32[2,1024,512]{2,1,0:T(8,128)S(1)} %get-tuple-element.347, f32[256,8192]{1,0:T(8,128)} %get-tuple-element.383, s32[]{:T(128)S(6)} %select_n.28, f32[256,512]{1,0:T(8,128)S(1)} %get-tuple-element.365, pred[]{:T(512)S(6)} %compare.3), kind=kOutput, calls=%fused_computation.8.clone.1 | convolution fusion | flops 1610874880 | bytes 4194309 | tf_op jit(solution)/shard_map/while/body/eval_jaxpr/dot_general | solution.py:39
  242.5 0.1 broadcast_add_fusion.2
  242.6 1.9 multiply_reduce_fusion.3
  244.5 3.3 %fusion.17 = f32[256,512]{1,0:T(8,128)S(1)} fusion(f32[2,1024,512]{2,1,0:T(8,128)S(1)} %get-tuple-element.347, f32[256,8192]{1,0:T(8,128)} %get-tuple-element.389, s32[]{:T(128)S(6)} %select_n.28, f32[256,512]{1,0:T(8,128)S(1)} %get-tuple-element.366, pred[]{:T(512)S(6)} %compare.3), kind=kOutput, calls=%fused_computation.9.clone.1 | convolution fusion | flops 1610874880 | bytes 4194309 | tf_op jit(solution)/shard_map/while/body/eval_jaxpr/dot_general | solution.py:42
  247.7 3.3 %fusion.16 = f32[256,512]{1,0:T(8,128)S(1)} fusion(f32[2,1024,512]{2,1,0:T(8,128)S(1)} %get-tuple-element.347, f32[256,8192]{1,0:T(8,128)} %get-tuple-element.383, s32[]{:T(128)S(6)} %select_n.28, f32[256,512]{1,0:T(8,128)S(1)} %get-tuple-element.365, pred[]{:T(512)S(6)} %compare.3), kind=kOutput, calls=%fused_computation.8.clone.1 | convolution fusion | flops 1610874880 | bytes 4194309 | tf_op jit(solution)/shard_map/while/body/eval_jaxpr/dot_general | solution.py:39
  251.0 0.1 broadcast_add_fusion.2
  251.1 1.9 multiply_reduce_fusion.3
  253.0 3.3 %fusion.17 = f32[256,512]{1,0:T(8,128)S(1)} fusion(f32[2,1024,512]{2,1,0:T(8,128)S(1)} %get-tuple-element.347, f32[256,8192]{1,0:T(8,128)} %get-tuple-element.389, s32[]{:T(128)S(6)} %select_n.28, f32[256,512]{1,0:T(8,128)S(1)} %get-tuple-element.366, pred[]{:T(512)S(6)} %compare.3), kind=kOutput, calls=%fused_computation.9.clone.1 | convolution fusion | flops 1610874880 | bytes 4194309 | tf_op jit(solution)/shard_map/while/body/eval_jaxpr/dot_general | solution.py:42
  256.3 3.3 %fusion.16 = f32[256,512]{1,0:T(8,128)S(1)} fusion(f32[2,1024,512]{2,1,0:T(8,128)S(1)} %get-tuple-element.347, f32[256,8192]{1,0:T(8,128)} %get-tuple-element.383, s32[]{:T(128)S(6)} %select_n.28, f32[256,512]{1,0:T(8,128)S(1)} %get-tuple-element.365, pred[]{:T(512)S(6)} %compare.3), kind=kOutput, calls=%fused_computation.8.clone.1 | convolution fusion | flops 1610874880 | bytes 4194309 | tf_op jit(solution)/shard_map/while/body/eval_jaxpr/dot_general | solution.py:39
  259.6 0.1 broadcast_add_fusion.2
  259.6 1.9 multiply_reduce_fusion.3
  261.5 3.3 %fusion.17 = f32[256,512]{1,0:T(8,128)S(1)} fusion(f32[2,1024,512]{2,1,0:T(8,128)S(1)} %get-tuple-element.347, f32[256,8192]{1,0:T(8,128)} %get-tuple-element.389, s32[]{:T(128)S(6)} %select_n.28, f32[256,512]{1,0:T(8,128)S(1)} %get-tuple-element.366, pred[]{:T(512)S(6)} %compare.3), kind=kOutput, calls=%fused_computation.9.clone.1 | convolution fusion | flops 1610874880 | bytes 4194309 | tf_op jit(solution)/shard_map/while/body/eval_jaxpr/dot_general | solution.py:42
  264.8 3.3 %fusion.16 = f32[256,512]{1,0:T(8,128)S(1)} fusion(f32[2,1024,512]{2,1,0:T(8,128)S(1)} %get-tuple-element.347, f32[256,8192]{1,0:T(8,128)} %get-tuple-element.383, s32[]{:T(128)S(6)} %select_n.28, f32[256,512]{1,0:T(8,128)S(1)} %get-tuple-element.365, pred[]{:T(512)S(6)} %compare.3), kind=kOutput, calls=%fused_computation.8.clone.1 | convolution fusion | flops 1610874880 | bytes 4194309 | tf_op jit(solution)/shard_map/while/body/eval_jaxpr/dot_general | solution.py:39
  268.1 0.1 broadcast_add_fusion.2
  268.2 1.9 multiply_reduce_fusion.3
  270.1 3.3 %fusion.17 = f32[256,512]{1,0:T(8,128)S(1)} fusion(f32[2,1024,512]{2,1,0:T(8,128)S(1)} %get-tuple-element.347, f32[256,8192]{1,0:T(8,128)} %get-tuple-element.389, s32[]{:T(128)S(6)} %select_n.28, f32[256,512]{1,0:T(8,128)S(1)} %get-tuple-element.366, pred[]{:T(512)S(6)} %compare.3), kind=kOutput, calls=%fused_computation.9.clone.1 | convolution fusion | flops 1610874880 | bytes 4194309 | tf_op jit(solution)/shard_map/while/body/eval_jaxpr/dot_general | solution.py:42
  273.3 3.3 %fusion.16 = f32[256,512]{1,0:T(8,128)S(1)} fusion(f32[2,1024,512]{2,1,0:T(8,128)S(1)} %get-tuple-element.347, f32[256,8192]{1,0:T(8,128)} %get-tuple-element.383, s32[]{:T(128)S(6)} %select_n.28, f32[256,512]{1,0:T(8,128)S(1)} %get-tuple-element.365, pred[]{:T(512)S(6)} %compare.3), kind=kOutput, calls=%fused_computation.8.clone.1 | convolution fusion | flops 1610874880 | bytes 4194309 | tf_op jit(solution)/shard_map/while/body/eval_jaxpr/dot_general | solution.py:39
  276.6 0.1 broadcast_add_fusion.2
  276.7 1.9 multiply_reduce_fusion.3
  278.6 3.3 %fusion.17 = f32[256,512]{1,0:T(8,128)S(1)} fusion(f32[2,1024,512]{2,1,0:T(8,128)S(1)} %get-tuple-element.347, f32[256,8192]{1,0:T(8,128)} %get-tuple-element.389, s32[]{:T(128)S(6)} %select_n.28, f32[256,512]{1,0:T(8,128)S(1)} %get-tuple-element.366, pred[]{:T(512)S(6)} %compare.3), kind=kOutput, calls=%fused_computation.9.clone.1 | convolution fusion | flops 1610874880 | bytes 4194309 | tf_op jit(solution)/shard_map/while/body/eval_jaxpr/dot_general | solution.py:42
  281.9 3.3 %fusion.16 = f32[256,512]{1,0:T(8,128)S(1)} fusion(f32[2,1024,512]{2,1,0:T(8,128)S(1)} %get-tuple-element.347, f32[256,8192]{1,0:T(8,128)} %get-tuple-element.383, s32[]{:T(128)S(6)} %select_n.28, f32[256,512]{1,0:T(8,128)S(1)} %get-tuple-element.365, pred[]{:T(512)S(6)} %compare.3), kind=kOutput, calls=%fused_computation.8.clone.1 | convolution fusion | flops 1610874880 | bytes 4194309 | tf_op jit(solution)/shard_map/while/body/eval_jaxpr/dot_general | solution.py:39
  285.2 0.7 rsqrt_select_fusion
  285.8 0.1 multiply_bitcast_fusion.1
  286.0 1.1 multiply_reduce_fusion.1
  287.1 15.6 %psum.7 = f32[512]{0:T(512)S(1)} all-reduce(f32[512]{0:T(512)S(1)} %get-tuple-element.266), channel_id=1, replica_groups=mesh['row'=8,'col'=32] {'row'}, use_global_device_ids=true, to_apply=%region_4.5 | all-reduce | flops 512 | bytes 4096 | tf_op jit(solution)/shard_map/psum | solution.py:56
  302.7 0.6 broadcast_multiply_fusion
  (35 shorter events, 0.2 us)
Async XLA Ops:
  7.2 106.8 %all-gather.3.cloned.1.call-start = ((), (), s32[]{:S(2)}) async-start(), calls=%async_computation | async-start | bytes 8650752 | tf_op jit(solution)/shard_map/all_gather | solution.py:23
  7.9 209.0 %all-gather.5.cloned.1.call-start = ((), (), s32[]{:S(2)}) async-start(), calls=%async_computation.1 | async-start | bytes 8650752 | tf_op jit(solution)/shard_map/all_gather | solution.py:24
Sparse Core Ops, SparseCore 0:
  10.4 103.4 all-gather.2
  116.4 100.4 all-gather.4
where the time goes:
time: 311 us; the launch traced here: 310 us
  waiting for transfers between devices  127 us (41%)
  blocking collectives  96.3 us (31%)
  matrix products  52.1 us (17%)
  other arithmetic  19.7 us (6%)
  between operations  14.1 us (5%)
    all_gather x1, waiting for transfers between devices, local(): lax.all_gather(lower_panel, 'col', axis=1, tiled=True)  103 us
    all_gather x1, blocking collectives, local(): lax.all_gather(weighted, 'col', axis=1, tiled=True)  41.5 us
    all_gather x1, blocking collectives, local(): lax.all_gather(pole_values, 'col', axis=1, tiled=True)  39.2 us
    dot_general x8, matrix products, advance(): jnp.dot(window[0], basis_tile[0], precision=exact_mode, preferred_element...  26 us
    dot_general x8, matrix products, advance(): jnp.dot(window[1], basis_tile[1], precision=exact_mode, preferred_element...  26 us
    all_gather x1, waiting for transfers between devices, local(): lax.all_gather(upper_panel, 'col', axis=1, tiled=True)  23.1 us
    psum x1, blocking collectives, local(): lax.psum(partial_weight, 'row') / (2 * rows_here * lax.axis_size('row'))  15.6 us
    reduce_sum x8, other arithmetic, advance(): jnp.sum(cauchy * cauchy, axis=(0, 1))  15 us
  transfers between devices with their start and end apart: 2, of which 2 were waited for; matrix products, arithmetic and copies ran while one was open for 0% of the time, Pallas kernels for 0%

commit v1 on v0

--- a/solution.py
+++ b/solution.py
@@ -20,7 +20,9 @@
     child_base = jnp.array([0, N1], jnp.int32)
     zeros_acc = jnp.zeros((rows_here, own_cols), jnp.float32)
     pieces = (
-        lax.all_gather(upper_panel, "col", axis=1, tiled=True),
+        jnp.concatenate(
+            lax.all_to_all(jnp.stack([upper_panel] * lax.axis_size("col")), "col", 0, 0), axis=1
+        ),
         lax.all_gather(lower_panel, "col", axis=1, tiled=True),
         lax.all_gather(pole_values, "col", axis=1, tiled=True),
         lax.all_gather(weighted, "col", axis=1, tiled=True),

time: 311 us -> 448 us (1.44)
  blocking collectives: 96.3 us -> 319 us
  waiting for transfers between devices: 127 us -> 0.68 us
  local copies, waits for them, and re-layouts: 0.02 us -> 14.2 us
  starting transfers between devices: 0.08 us -> 12.3 us
  other arithmetic: 19.7 us -> 27.5 us
  matrix products: 52.1 us -> 58.5 us
    all_gather x1, blocking collectives: 41.5 us -> 250 us  [local(): lax.all_gather(weighted, 'col', axis=1, tiled=True)]
    all_gather x1, waiting for transfers between devices: 103 us -> 0.01 us  [local(): lax.all_gather(lower_panel, 'col', axis=1, tiled=True)]
    all_gather x1 -> x0, waiting for transfers between devices: 23.1 us -> none  [local(): lax.all_gather(upper_panel, 'col', axis=1, tiled=True)]
    psum x1, blocking collectives: 15.6 us -> 32.6 us  [local(): lax.psum(partial_weight, 'row') / (2 * rows_here * lax.axis_size('row'))]
    all_to_all x0 -> x1, starting transfers between devices: none -> 12.3 us  [local(): lax.all_to_all(jnp.stack([upper_panel] * lax.axis_size('col')), 'col', 0, 0)]
    reduce_sum x8, other arithmetic: 15 us -> 24.9 us  [advance(): jnp.sum(cauchy * cauchy, axis=(0, 1))]
    all_to_all x0 -> x1, local copies, waits for them, and re-layouts: none -> 8.94 us  [local(): lax.all_to_all(jnp.stack([upper_panel] * lax.axis_size('col')), 'col', 0, 0)]
    dot_general x8, matrix products: 26 us -> 32.5 us  [advance(): jnp.dot(window[1], basis_tile[1], precision=exact_mode, preferred_element...]
  transfers between devices with their start and end apart: 2 -> 2, of which waited for: 2 -> 0; matrix products, arithmetic and copies ran while one was open for 0% -> 2% of each run, Pallas kernels for 0% -> 0%
where the time goes in v1:
time: 448 us; the launch traced here: 447 us
  blocking collectives  319 us (71%)
  matrix products  58.5 us (13%)
  other arithmetic  27.5 us (6%)
  local copies, waits for them, and re-layouts  14.2 us (3%)
  between operations  14.1 us (3%)
  starting transfers between devices  12.3 us (3%)
    all_gather x1, blocking collectives, local(): lax.all_gather(weighted, 'col', axis=1, tiled=True)  250 us
    all_gather x1, blocking collectives, local(): lax.all_gather(pole_values, 'col', axis=1, tiled=True)  36.8 us
    psum x1, blocking collectives, local(): lax.psum(partial_weight, 'row') / (2 * rows_here * lax.axis_size('row'))  32.6 us
    dot_general x8, matrix products, advance(): jnp.dot(window[1], basis_tile[1], precision=exact_mode, preferred_element...  32.5 us
    dot_general x8, matrix products, advance(): jnp.dot(window[0], basis_tile[0], precision=exact_mode, preferred_element...  26 us
    reduce_sum x8, other arithmetic, advance(): jnp.sum(cauchy * cauchy, axis=(0, 1))  24.9 us
    all_to_all x1, starting transfers between devices, local(): lax.all_to_all(jnp.stack([upper_panel] * lax.axis_size('col')), 'col', 0, 0)  12.3 us
  transfers between devices with their start and end apart: 2, of which 0 were waited for; matrix products, arithmetic and copies ran while one was open for 2% of the time, Pallas kernels for 0%

profile of v1, /device:TPU:1, one launch (start us, length us, event | category | flops | bytes accessed | tf_op | source)
XLA Modules:
  0.0 446.9 jit_solution(10430833083388205625)
XLA Ops:
  7.2 5.1 %stack.8 = f32[32,256,256]{2,1,0:T(8,128)} broadcast(f32[256,256]{1,0:T(8,128)} %param.10), dimensions={1,2} | broadcast | bytes 8650752 | tf_op jit(solution)/shard_map/stack | solution.py:24
  12.3 12.3 %all-to-all-start = ((f32[32,256,256]{2,1,0:T(8,128)}), f32[32,256,256]{2,1,0:T(8,128)}, u32[]{:S(2)}, u32[]{:S(2)}) async-start(f32[32,256,256]{2,1,0:T(8,128)} %stack.8), calls=%async_computation | async-start | bytes 16777216 | tf_op jit(solution)/shard_map/all_to_all | solution.py:24
  24.6 0.0 all-gather.2.cloned.1.call-start
  24.6 0.7 all-gather.2.cloned.1.call-update
  25.4 249.6 %all_gather.9 = f32[2,8192]{1,0:T(2,128)S(1)} all-gather(f32[2,256]{1,0:T(2,128)S(1)} %convert_multiply_fusion), channel_id=1, replica_groups=mesh['row'=8,'col'=32] {'col'}, dimensions={1}, use_global_device_ids=true | all-gather | bytes 67584 | tf_op jit(solution)/shard_map/all_gather | solution.py:28
  275.0 36.8 %all_gather.10 = f32[2,8192]{1,0:T(2,128)S(1)} all-gather(f32[2,256]{1,0:T(2,128)S(1)} %copy-done.5), channel_id=1, replica_groups=mesh['row'=8,'col'=32] {'col'}, dimensions={1}, use_global_device_ids=true | all-gather | bytes 67584 | tf_op jit(solution)/shard_map/all_gather | solution.py:27
  311.9 0.0 copy-start.2
  311.9 0.0 all-to-all-done
  311.9 8.9 %copy.12 = f32[32,256,256]{1,2,0:T(8,128)} copy(f32[32,256,256]{2,1,0:T(8,128)} %all-to-all-done) | data formatting | bytes 16777216 | tf_op jit(solution)/shard_map/all_to_all | solution.py:24
  320.8 84.8 %while.18 = (s32[]{:T(128)}, f32[256,512]{1,0:T(8,128)S(1)}, f32[256,512]{1,0:T(8,128)S(1)}, f32[512]{0:T(512)S(1)}, f32[256,8192]{0,1:T(8,128)}, /*index=5*/pre...) while((s32[]{:T(128)}, f32[256,512]{1,0:T(8,128)S(1)}, ...), condition=%wide.region_2.3_spmd.clone, body=%wide.region_0.2_spmd.clone.sunk | while | flops 3229093376 | bytes 29446912 | solution.py:49
  320.9 0.1 broadcast_add_fusion.2
  320.9 3.1 multiply_reduce_fusion.3
  324.0 4.1 fusion.17
  328.1 3.3 fusion.16
  331.5 0.1 broadcast_add_fusion.2
  331.5 3.1 multiply_reduce_fusion.3
  334.6 4.1 fusion.17
  338.7 3.3 fusion.16
  342.1 0.1 broadcast_add_fusion.2
  342.1 3.1 multiply_reduce_fusion.3
  345.3 4.1 fusion.17
  349.3 3.3 fusion.16
  352.7 0.1 broadcast_add_fusion.2
  352.7 3.1 multiply_reduce_fusion.3
  355.9 4.1 fusion.17
  359.9 3.3 fusion.16
  363.3 0.1 broadcast_add_fusion.2
  363.3 3.1 multiply_reduce_fusion.3
  366.5 4.1 fusion.17
  370.5 0.0 copy-done
  370.5 3.3 fusion.16
  373.9 0.1 broadcast_add_fusion.2
  374.0 3.1 multiply_reduce_fusion.3
  377.1 4.1 fusion.17
  381.1 0.0 copy-done
  381.1 3.3 fusion.16
  384.5 0.1 broadcast_add_fusion.2
  384.6 3.1 multiply_reduce_fusion.3
  387.7 4.1 fusion.17
  391.7 3.3 fusion.16
  395.1 0.1 broadcast_add_fusion.2
  395.2 3.1 multiply_reduce_fusion.3
  398.3 4.1 fusion.17
  402.4 3.3 fusion.16
  405.7 0.1 multiply_bitcast_fusion.1
  405.8 1.1 multiply_reduce_fusion.1
  406.9 32.6 %psum.7 = f32[512]{0:T(512)S(1)} all-reduce(f32[512]{0:T(512)S(1)} %get-tuple-element.288), channel_id=1, replica_groups=mesh['row'=8,'col'=32] {'row'}, use_global_device_ids=true, to_apply=%region_4.5 | all-reduce | flops 512 | bytes 4096 | tf_op jit(solution)/shard_map/psum | solution.py:58
  439.5 0.6 broadcast_multiply_fusion
  (62 shorter events, 0.3 us)
Async XLA Ops:
  12.3 13.1 %copy-start.3 = (f32[2,256]{1,0:T(2,128)S(1)}, f32[2,256]{1,0:T(2,128)}, u32[]{:S(2)}) copy-start(f32[2,256]{1,0:T(2,128)} %param.13) | copy-start | bytes 6148
  12.3 13.1 %copy-start.4 = (s32[2,256]{1,0:T(2,128)S(1)}, s32[2,256]{1,0:T(2,128)}, u32[]{:S(2)}) copy-start(s32[2,256]{1,0:T(2,128)} %param.14) | copy-start | bytes 6148
  12.3 262.8 %copy-start.5 = (f32[2,256]{1,0:T(2,128)S(1)}, f32[2,256]{1,0:T(2,128)}, u32[]{:S(2)}) copy-start(f32[2,256]{1,0:T(2,128)} %param.12) | copy-start | bytes 6148
  12.3 299.6 %copy-start.1 = (s32[512]{0:T(512)S(1)}, s32[512]{0:T(512)}, u32[]{:S(2)}) copy-start(s32[512]{0:T(512)} %param.16) | copy-start | bytes 6148
  12.3 299.6 %all-to-all-start = ((f32[32,256,256]{2,1,0:T(8,128)}), f32[32,256,256]{2,1,0:T(8,128)}, u32[]{:S(2)}, u32[]{:S(2)}) async-start(f32[32,256,256]{2,1,0:T(8,128)} %stack.8), calls=%async_computation | async-start | bytes 16777216 | tf_op jit(solution)/shard_map/all_to_all | solution.py:24
  24.6 296.2 %all-gather.2.cloned.1.call-start = ((), (), s32[]{:S(2)}) async-start(), calls=%async_computation.1 | async-start | bytes 8650752 | tf_op jit(solution)/shard_map/all_gather | solution.py:26
  311.9 9.0 %copy-start.2 = (f32[512]{0:T(512)S(1)}, f32[512]{0:T(512)}, u32[]{:S(2)}) copy-start(f32[512]{0:T(512)} %param.15) | copy-start | bytes 6148
  324.0 4.1 copy-start
  334.6 4.1 copy-start
  345.3 4.1 copy-start
  355.9 4.1 copy-start
  366.5 4.1 copy-start
  377.1 4.1 copy-start
  387.7 4.1 copy-start
  398.3 4.1 copy-start
Sparse Core Ops, SparseCore 0:
  27.9 237.8 all-gather.1
